TPU v7x, 32 devices: a whole 2x2x4 slice. The times are simulated.
32 devices in a mesh: tile: 8 (over z, y), head: 4 (over x, core).
Axes of the slice: x: 2, y: 2, z: 4, core: 2. Of those that a mesh axis runs over, the one named last changes fastest.
Arguments:
- tokens: bfloat16 [256, 32768], P('head', 'tile'), may hold values from -6 to 6
- grad_in: bfloat16 [256, 32768], P('head', 'tile'), may hold values from -6 to 6
- w_qkv: bfloat16 [3, 256, 256], P(None, 'head'), may hold values from -0.375 to 0.375
- w_out: bfloat16 [256, 256], P('head'), may hold values from -0.375 to 0.375
- neighbors: int32 [9, 32768], P(None, 'tile'), may hold values from 0 to 4479, as said below
- send_rows: int32 [8, 3, 128], P('tile'), may hold values from 0 to 4096, as said below
Outputs:
- d_tokens: float32 [256, 32768], P('head', 'tile')
- grad_qkv: float32 [3, 256, 256], P(None, 'head')
- grad_out: float32 [256, 256], P('head')
Inputs may be any that keep to these rules, and one draw needn't show every extreme that they name: `send_rows`: entries of list p of index d are rows of index d, live entries first, the rest equal to 4096; list 2 of every index is full, and list 0 of index 0 is half full. `neighbors`: slot 0 of row r of an index is r itself; an entry below 4096 lies within 64 rows of r, counted around the index's 4096 rows; every entry at or above 4096 points to a live entry of the list it names.
All inputs are finite; a program needn't handle non-finite values.
Results may differ from a plain program's by a relative error of at most 0.0059.
Values may be sent and summed in bfloat16 or wider, within the bound.
A program may use at most 64 MiB of HBM per device.

v0:
```python
import math

import jax
import jax.numpy as jnp
from jax import lax
from jax.sharding import PartitionSpec as P

C = 256
HEADS = 8
NBR = 9
TILE_PIX = 64


def with_halo(value, sides, width):
    for axis, dim in sides:
        devices, length = (lax.axis_size(axis), value.shape[dim])
        up = [(i, (i + 1) % devices) for i in range(devices)]
        down = [(j, i) for i, j in up]
        last = lax.slice_in_dim(value, length - width, length, axis=dim)
        initial = lax.slice_in_dim(value, 0, width, axis=dim)
        before = lax.ppermute(last, axis, up)
        after = lax.ppermute(initial, axis, down)
        value = jnp.concatenate([before, value, after], axis=dim)
    return value


def passed_along(value, axis, steps):
    count = lax.axis_size(axis)
    pairs = [(source, (source + steps) % count) for source in range(count)]
    return lax.ppermute(value, axis, pairs)


def attention(extended, picks_all, query, grad_att, block_rows):
    channels = query.shape[0]
    row_count = query.shape[1]
    head_dim = C // HEADS
    local_heads = channels // head_dim
    score_scale = 1.0 / math.sqrt(head_dim)
    block_count = row_count // block_rows
    pick_blocks = picks_all.reshape(NBR, block_count, block_rows).transpose(1, 0, 2)
    query_blocks = query.reshape(channels, block_count, block_rows).transpose(1, 0, 2)
    dout_blocks = grad_att.reshape(channels, block_count, block_rows).transpose(1, 0, 2)

    def attend_block(totals, inputs):
        picks, query_rows, dout_rows = inputs
        near = extended[picks].astype(jnp.float32)
        near_keys = near[:, :, :channels].reshape(NBR, block_rows, local_heads, head_dim)
        near_values = near[:, :, channels:].reshape(NBR, block_rows, local_heads, head_dim)
        query_heads = query_rows.astype(jnp.float32).T.reshape(block_rows, local_heads, head_dim)
        dout_heads = dout_rows.T.reshape(block_rows, local_heads, head_dim)
        scores = jnp.einsum("rhd,jrhd->jrh", query_heads, near_keys) * score_scale
        expon = jnp.exp(scores)
        probs = expon / jnp.sum(expon, axis=0)
        attended = jnp.einsum("jrh,jrhd->rhd", probs, near_values)
        dprob = jnp.einsum("rhd,jrhd->jrh", dout_heads, near_values)
        dscore = probs * (dprob - jnp.sum(probs * dprob, axis=0))
        grad_query = jnp.einsum("jrh,jrhd->rhd", dscore, near_keys) * score_scale
        grad_keys = dscore[..., None] * query_heads[None] * score_scale
        grad_values = probs[..., None] * dout_heads[None]
        grad_near = jnp.concatenate(
            [
                grad_keys.reshape(NBR, block_rows, channels),
                grad_values.reshape(NBR, block_rows, channels),
            ],
            axis=2,
        )
        totals = totals.at[picks.reshape(-1)].add(grad_near.reshape(NBR * block_rows, 2 * channels))
        attended_cols = attended.reshape(block_rows, channels).astype(jnp.bfloat16).T
        query_cols = grad_query.reshape(block_rows, channels).T
        return (totals, (attended_cols, query_cols))

    start_grad = jnp.zeros((extended.shape[0], 2 * channels), jnp.float32)
    grad_ext, (attended, grad_query) = lax.scan(
        attend_block, start_grad, (pick_blocks, query_blocks, dout_blocks)
    )
    attended = attended.transpose(1, 0, 2).reshape(channels, row_count)
    grad_query = grad_query.transpose(1, 0, 2).reshape(channels, row_count)
    return (grad_ext, attended, grad_query)


def local(tokens, grad_in, w_qkv, w_out, neighbors, send_rows):
    groups = lax.axis_size("tile")
    border = send_rows.shape[2]
    offsets = (1, groups - 1, groups // 2)
    lists = send_rows[0]
    head_count = lax.axis_size("head")
    row_part = lax.axis_index("head")
    full_rows = tokens.shape[1]
    rows_x, rows_dy = (
        lax.all_to_all(tokens, "head", split_axis=1, concat_axis=0, tiled=True),
        lax.all_to_all(grad_in, "head", split_axis=1, concat_axis=0, tiled=True),
    )
    w_all, wo_all = (
        lax.all_gather(w_qkv, "head", axis=1, tiled=True),
        lax.all_gather(w_out, "head", axis=0, tiled=True),
    )
    quarter = rows_x.shape[1]
    margin = TILE_PIX
    projected = jnp.einsum("tnc,cr->tnr", w_all, rows_x, preferred_element_type=jnp.float32).astype(
        jnp.bfloat16
    )
    query = projected[0]
    packed = jnp.concatenate([projected[1].T, projected[2].T], axis=1)
    framed = with_halo(packed, (("head", 0),), margin)
    start_row = row_part * quarter
    within = lists - start_row
    is_owned = (within >= 0) & (within < quarter)
    clipped = jnp.clip(within, 0, quarter - 1)
    own_lists = jnp.where(is_owned[..., None], packed[clipped].astype(jnp.float32), 0.0)
    joined = lax.psum(own_lists.astype(jnp.bfloat16), "head")
    pieces = []
    for peer in range(3):
        pieces.append(passed_along(joined[peer], "tile", offsets[peer]))
    halo = jnp.stack(pieces)
    extended = jnp.concatenate([framed, halo.reshape(3 * border, 2 * C)], axis=0)
    near_ids = lax.dynamic_slice_in_dim(neighbors, start_row, quarter, 1)
    picks = jnp.where(
        near_ids < full_rows,
        (near_ids - start_row + margin) % full_rows,
        near_ids - full_rows + quarter + 2 * margin,
    )
    grad_att = jnp.dot(wo_all, rows_dy, preferred_element_type=jnp.float32)
    grad_ext, attended, grad_query = attention(extended, picks, query, grad_att, min(512, quarter))
    from_above = passed_along(grad_ext[:margin], "head", head_count - 1)
    from_below = passed_along(grad_ext[quarter + margin : quarter + 2 * margin], "head", 1)
    own_grad = grad_ext[margin : margin + quarter]
    own_grad = own_grad.at[:margin].add(from_below)
    own_grad = own_grad.at[quarter - margin :].add(from_above)
    grad_halo = grad_ext[quarter + 2 * margin :].reshape(3, border, 2 * C)
    answers = []
    for peer in range(3):
        answers.append(passed_along(grad_halo[peer], "tile", (groups - offsets[peer]) % groups))
    backward = lax.psum(jnp.stack(answers), "head")
    targets = jnp.where(is_owned, within, quarter)
    own_grad = jnp.concatenate([own_grad, jnp.zeros((1, 2 * C), jnp.float32)], axis=0)
    own_grad = own_grad.at[targets.reshape(-1)].add(backward.reshape(3 * border, 2 * C))[:quarter]
    grad_proj = jnp.stack([grad_query, own_grad[:, :C].T, own_grad[:, C:].T]).astype(jnp.bfloat16)
    grad_scale = 1.0 / math.sqrt(full_rows * groups)
    part_qkv = (
        jnp.einsum("tnr,cr->tnc", grad_proj, rows_x, preferred_element_type=jnp.float32)
        * grad_scale
    )
    part_out = (
        lax.dot_general(
            attended, rows_dy, (((1,), (1,)), ((), ())), preferred_element_type=jnp.float32
        )
        * grad_scale
    )
    total_qkv, total_out = lax.psum((part_qkv, part_out), ("tile", "head"))
    share_cols = C // head_count
    grad_qkv = lax.dynamic_slice_in_dim(total_qkv, row_part * share_cols, share_cols, 1)
    grad_out = lax.dynamic_slice_in_dim(total_out, row_part * share_cols, share_cols, 0)
    mixed = jnp.einsum(
        "tnc,tnr->cr", w_all, grad_proj, preferred_element_type=jnp.float32
    ) + rows_dy.astype(jnp.float32)
    d_tokens = lax.all_to_all(mixed, "head", split_axis=0, concat_axis=1, tiled=True)
    return (d_tokens, grad_qkv, grad_out)


def solution(mesh):
    return jax.shard_map(
        local,
        mesh=mesh,
        in_specs=(
            P("head", "tile"),
            P("head", "tile"),
            P(None, "head", None),
            P("head", None),
            P(None, "tile"),
            P("tile", None, None),
        ),
        out_specs=(P("head", "tile"), P(None, "head", None), P("head", None)),
        check_vma=False,
    )
```

profile of v0, /device:TPU:0, one launch (start us, length us, event | category | flops | bytes accessed | tf_op | source)
XLA Modules:
  0.0 585.2 jit_solution(4869772585306750288)
XLA Ops:
  7.2 1.9 copy.132
  9.1 4.2 all-to-all-start
  14.0 1.9 copy.131
  16.0 9.2 %all_gather.6 = bf16[3,256,256]{2,1,0:T(8,128)(2,1)S(1)} all-gather(bf16[3,64,256]{2,1,0:T(8,128)(2,1)S(1)} %copy-done.18), channel_id=1, replica_groups=mesh['tile'=8,'head'=4] {'head'}, dimensions={1}, use_global_device_ids=true | all-gather | bytes 491520 | tf_op jit(solution)/shard_map/all_gather | solution.py:94
  25.1 3.5 all-to-all-start.1
  31.6 2.1 gather_fusion.1
  35.6 5.7 all_gather.7
  42.1 27.8 %all-reduce.6.cloned.1.call-done = bf16[3,128,512]{2,1,0:T(8,128)(2,1)} async-done(((bf16[3,128,512]{2,1,0:T(8,128)(2,1)}), bf16[3,128,512]{2,1,0:T(8,128)(2,1)}) %all-reduce.6.cloned.1.call-update) | async-done | bytes 393232 | tf_op jit(solution)/shard_map/psum | solution.py:110
  73.1 2.4 collective-permute-start.4
  75.5 2.3 collective-permute-start.3
  83.5 2.1 collective-permute-done.1
  86.5 2.4 concatenate.18
  88.9 2.6 copy.54
  91.9 274.4 %while.16 = (s32[]{:T(128)}, f32[1536,512]{1,0:T(8,128)S(1)}, bf16[2,256,512]{1,2,0:T(8,128)(2,1)}, bf16[2,256,512]{2,1,0:T(8,128)(2,1)}, s32[2,9,512]{2,0,1:T(2...) while((s32[]{:T(128)}, f32[1536,512]{1,0:T(8,128)S(1)}, ...), condition=%wide.region_5.6_spmd, body=%wide.region_1.5_spmd.sunk | while | flops 22863888 | bytes 245811632 | solution.py:73
  92.8 1.9 fusion.55
  94.7 2.1 copy.159
  101.3 2.1 copy.163
  103.4 3.6 mul.129
  107.0 6.1 %copy.164 = f32[4608,256]{0,1:T(8,128)} copy(f32[4608,256]{1,0:T(8,128)} %bitcast.225) | data formatting | bytes 9437184 | tf_op jit(solution)/shard_map/while/body/eval_jaxpr/mul | solution.py:58
  113.1 3.7 mul.126
  116.8 6.1 %copy.160 = f32[4608,256]{0,1:T(8,128)} copy(f32[4608,256]{1,0:T(8,128)} %bitcast.226) | data formatting | bytes 9437184 | tf_op jit(solution)/shard_map/while/body/eval_jaxpr/mul | solution.py:59
  122.8 15.6 %gather_fusion = bf16[4608,512]{1,0:T(8,128)(2,1)} fusion(bf16[1536,512]{1,0:T(8,128)(2,1)} %get-tuple-element.215, s32[5120]{0:T(1024)S(1)} %pad_clamp_fusion.3), kind=kCustom, calls=%fused_computation.clone.1 | custom fusion | bytes 9455616 | tf_op jit(solution)/shard_map/while/body/eval_jaxpr/gather | solution.py:46
  138.4 4.9 fusion.54
  143.3 4.3 copy.157
  147.6 2.7 multiply_reduce_fusion.8
  152.4 4.3 copy.161
  156.7 2.8 multiply_reduce_fusion.9
  159.6 2.2 multiply_reduce_fusion.10
  164.9 2.3 multiply_reduce_fusion.11
  170.0 4.5 copy.158
  176.1 4.5 copy.162
  180.7 2.9 multiply_multiply_fusion.2
  183.6 6.6 %pad_maximum_fusion.8 = f32[4608,512]{0,1:T(8,128)} fusion(f32[4608,256]{0,1:T(8,128)S(1)} %mul.127, f32[4608,256]{0,1:T(8,128)} %multiply_multiply_fusion.2), kind=kLoop, calls=%fused_computation.4.clone.1 | loop fusion | flops 2359296 | bytes 18874368 | tf_op jit(solution)/shard_map/while/body/eval_jaxpr/concatenate | solution.py:60
  190.2 9.6 %copy.165 = f32[4608,512]{1,0:T(8,128)} copy(f32[4608,512]{0,1:T(8,128)} %pad_maximum_fusion.8) | data formatting | bytes 18874368 | tf_op jit(solution)/shard_map/while/body/eval_jaxpr/concatenate | solution.py:60
  199.8 29.3 %scatter_fusion = f32[1536,512]{1,0:T(8,128)S(1)} fusion(f32[1536,512]{1,0:T(8,128)S(1)} %get-tuple-element.202, s32[4608]{0:T(1024)S(1)} %copy-done.8, f32[4608,512]{1,0:T(8,128)} %copy.165), kind=kCustom, calls=%fused_computation.2.clone.1 | custom fusion | flops 2359296 | bytes 28329984 | tf_op jit(solution)/shard_map/while/body/eval_jaxpr/scatter-add | solution.py:67
  231.7 2.1 copy.159
  238.3 2.1 copy.163
  240.4 3.6 mul.129
  244.0 6.1 %copy.164 = f32[4608,256]{0,1:T(8,128)} copy(f32[4608,256]{1,0:T(8,128)} %bitcast.225) | data formatting | bytes 9437184 | tf_op jit(solution)/shard_map/while/body/eval_jaxpr/mul | solution.py:58
  250.1 3.7 mul.126
  253.8 6.1 %copy.160 = f32[4608,256]{0,1:T(8,128)} copy(f32[4608,256]{1,0:T(8,128)} %bitcast.226) | data formatting | bytes 9437184 | tf_op jit(solution)/shard_map/while/body/eval_jaxpr/mul | solution.py:59
  259.8 15.6 %gather_fusion = bf16[4608,512]{1,0:T(8,128)(2,1)} fusion(bf16[1536,512]{1,0:T(8,128)(2,1)} %get-tuple-element.215, s32[5120]{0:T(1024)S(1)} %pad_clamp_fusion.3), kind=kCustom, calls=%fused_computation.clone.1 | custom fusion | bytes 9455616 | tf_op jit(solution)/shard_map/while/body/eval_jaxpr/gather | solution.py:46
  275.4 4.9 fusion.54
  280.3 4.3 copy.157
  284.6 2.7 multiply_reduce_fusion.8
  289.4 4.3 copy.161
  293.7 2.8 multiply_reduce_fusion.9
  296.6 2.2 multiply_reduce_fusion.10
  301.9 2.3 multiply_reduce_fusion.11
  307.0 4.5 copy.158
  313.1 4.5 copy.162
  317.7 2.9 multiply_multiply_fusion.2
  320.6 6.6 %pad_maximum_fusion.8 = f32[4608,512]{0,1:T(8,128)} fusion(f32[4608,256]{0,1:T(8,128)S(1)} %mul.127, f32[4608,256]{0,1:T(8,128)} %multiply_multiply_fusion.2), kind=kLoop, calls=%fused_computation.4.clone.1 | loop fusion | flops 2359296 | bytes 18874368 | tf_op jit(solution)/shard_map/while/body/eval_jaxpr/concatenate | solution.py:60
  327.2 9.6 %copy.165 = f32[4608,512]{1,0:T(8,128)} copy(f32[4608,512]{0,1:T(8,128)} %pad_maximum_fusion.8) | data formatting | bytes 18874368 | tf_op jit(solution)/shard_map/while/body/eval_jaxpr/concatenate | solution.py:60
  336.8 29.3 %scatter_fusion = f32[1536,512]{1,0:T(8,128)S(1)} fusion(f32[1536,512]{1,0:T(8,128)S(1)} %get-tuple-element.202, s32[4608]{0:T(1024)S(1)} %copy-done.8, f32[4608,512]{1,0:T(8,128)} %copy.165), kind=kCustom, calls=%fused_computation.2.clone.1 | custom fusion | flops 2359296 | bytes 28329984 | tf_op jit(solution)/shard_map/while/body/eval_jaxpr/scatter-add | solution.py:67
  373.0 2.2 stack_reshape.4
  375.7 2.2 convolution_multiply_fusion.1
  378.0 8.2 %collective-permute-done.9 = f32[128,512]{1,0:T(8,128)} collective-permute-done((f32[128,512]{1,0:T(8,128)}, f32[128,512]{1,0:T(8,128)}, u32[]{:S(2)}, u32[]{:S(2)}) %collective-permute-start.9) | collective-permute-done | bytes 262176 | tf_op jit(solution)/shard_map/ppermute | solution.py:30
  386.2 2.0 pad_maximum_fusion.3
  393.1 30.6 %all-reduce.8.cloned.1.call-done = f32[384,512]{1,0:T(8,128)} async-done(((f32[384,512]{1,0:T(8,128)}), f32[384,512]{1,0:T(8,128)}) %all-reduce.8.cloned.1.call-update) | async-done | bytes 786448 | tf_op jit(solution)/shard_map/psum | solution.py:133
  423.7 4.2 scatter_fusion.1
  432.4 3.5 all-to-all-start.2
  435.9 2.5 convolution_multiply_fusion
  438.5 136.1 %all-reduce.10.cloned.1.call-done = (f32[3,256,256]{2,1,0:T(8,128)}, f32[256,256]{1,0:T(8,128)}) async-done(((f32[3,256,256]{2,1,0:T(8,128)}, f32[256,256]{1,0:T(8,128)}), (f32[3,256,256]{2,1,0:T(8,128)}, f32[256,256]{1,0:T(8,128)})) %all-reduce.10.cloned.1.call-update) | async-done | bytes 1048592 | tf_op jit(solution)/shard_map/psum | solution.py:149
  (176 shorter events, 68.5 us)
Async XLA Ops:
  7.2 8.8 %copy-start.19 = (s32[1,3,128]{2,0,1:T(1,128)S(1)}, s32[1,3,128]{2,0,1:T(1,128)}, u32[]{:S(2)}) copy-start(s32[1,3,128]{2,0,1:T(1,128)} %param.17) | copy-start | bytes 4612
  7.2 8.8 %copy-start.18 = (bf16[3,64,256]{2,1,0:T(8,128)(2,1)S(1)}, bf16[3,64,256]{2,1,0:T(8,128)(2,1)}, u32[]{:S(2)}) copy-start(bf16[3,64,256]{2,1,0:T(8,128)(2,1)} %param.14) | copy-start | bytes 294916
  9.1 16.0 %all-to-all-start = ((bf16[64,4,1024]{2,0,1:T(8,128)(2,1)}), bf16[64,4,1024]{2,0,1:T(8,128)(2,1)S(1)}, u32[]{:S(2)}, u32[]{:S(2)}) async-start(bf16[64,4,1024]{2,0,1:T(8,128)(2,1)} %bitcast.161), calls=%async_computation | async-start | bytes 1048576 | tf_op jit(solution)/shard_map/all_to_all | solution.py:90
  25.1 5.0 copy-start.9
  25.1 5.0 copy-start.6
  25.1 16.8 %all-to-all-start.1 = ((bf16[64,4,1024]{2,0,1:T(8,128)(2,1)}), bf16[64,4,1024]{2,0,1:T(8,128)(2,1)S(1)}, u32[]{:S(2)}, u32[]{:S(2)}) async-start(bf16[64,4,1024]{2,0,1:T(8,128)(2,1)} %bitcast.160), calls=%async_computation.1 | async-start | bytes 1048576 | tf_op jit(solution)/shard_map/all_to_all | solution.py:91
  28.6 41.3 %all-reduce.6.cloned.1.call-start = ((), (), s32[]{:S(2)}) async-start(), calls=%async_computation.3 | async-start | bytes 786432 | tf_op jit(solution)/shard_map/psum | solution.py:110
  30.1 0.8 copy-start.4
  34.5 46.9 %copy-start.5 = (bf16[1024,256]{0,1:T(8,128)(2,1)S(1)}, bf16[1024,256]{0,1:T(8,128)(2,1)}, u32[]{:S(2)}) copy-start(bf16[1024,256]{0,1:T(8,128)(2,1)} %copy-done.4) | copy-start | bytes 1572868
  34.6 389.1 %all-reduce.8.cloned.1.call-start = ((), (), s32[]{:S(2)}) async-start(), calls=%async_computation.4 | async-start | bytes 1572864 | tf_op jit(solution)/shard_map/psum | solution.py:133
  41.9 39.7 %copy-start.2 = (bf16[64,4,1024]{2,0,1:T(8,128)(2,1)}, bf16[64,4,1024]{2,0,1:T(8,128)(2,1)S(1)}, u32[]{:S(2)}) copy-start(bf16[64,4,1024]{2,0,1:T(8,128)(2,1)S(1)} %all-to-all-done.1) | copy-start | bytes 1572868
  71.7 10.5 %collective-permute-start.2 = (bf16[128,512]{1,0:T(8,128)(2,1)}, bf16[128,512]{1,0:T(8,128)(2,1)}, u32[]{:S(2)}, u32[]{:S(2)}) collective-permute-start(bf16[128,512]{1,0:T(8,128)(2,1)} %get-tuple-element.132), channel_id=1, source_target_pairs={{0,4},{4,8},{8,12},{12,16},{16,20},{20,24},{24,28},{28,0},{1,5},{5... | collective-permute-start | bytes 393224 | tf_op jit(solution)/shard_map/ppermute | solution.py:30
  73.1 9.0 %collective-permute-start.4 = (bf16[128,512]{1,0:T(8,128)(2,1)}, bf16[128,512]{1,0:T(8,128)(2,1)}, u32[]{:S(2)}, u32[]{:S(2)}) collective-permute-start(bf16[128,512]{1,0:T(8,128)(2,1)} %get-tuple-element.133), channel_id=1, source_target_pairs={{0,16},{4,20},{8,24},{12,28},{16,0},{20,4},{24,8},{28,12},{1,17},{... | collective-permute-start | bytes 393224 | tf_op jit(solution)/shard_map/ppermute | solution.py:30
  75.5 6.6 %collective-permute-start.3 = (bf16[128,512]{1,0:T(8,128)(2,1)S(1)}, bf16[128,512]{1,0:T(8,128)(2,1)}, u32[]{:S(2)}, u32[]{:S(2)}) collective-permute-start(bf16[128,512]{1,0:T(8,128)(2,1)S(1)} %get-tuple-element.134), channel_id=1, source_target_pairs={{0,28},{4,0},{8,4},{12,8},{16,12},{20,16},{24,20},{28,24},{1,29},{... | collective-permute-start | bytes 393224 | tf_op jit(solution)/shard_map/ppermute | solution.py:30
  81.6 3.9 collective-permute-start.1
  81.7 4.8 collective-permute-start
  92.1 14.9 %copy-start.16 = (s32[2,9,512]{2,0,1:T(2,128)}, s32[2,9,512]{2,0,1:T(2,128)S(1)}, u32[]{:S(2)}) copy-start(s32[2,9,512]{2,0,1:T(2,128)S(1)} %get-tuple-element.214) | copy-start | bytes 110596 | tf_op jit(solution)/shard_map/while
  156.7 2.8 copy-start
  163.6 3.7 copy-start.11
  163.6 4.6 copy-start.1
  167.3 0.8 copy-start.12
  168.9 5.6 slice-start.2
  169.9 4.5 slice-start.3
  175.0 5.6 slice-start
  176.1 4.5 slice-start.1
  190.2 9.6 %copy-start.8 = (s32[4608]{0:T(1024)S(1)}, s32[4608]{0:T(1024)}, u32[]{:S(2)}) copy-start(s32[4608]{0:T(1024)} %fusion.53) | copy-start | bytes 55300 | tf_op jit(solution)/shard_map/while
  199.8 29.3 %copy-start.17 = (s32[2,9,512]{2,0,1:T(2,128)S(1)}, s32[2,9,512]{2,0,1:T(2,128)}, u32[]{:S(2)}) copy-start(s32[2,9,512]{2,0,1:T(2,128)} %copy-done.16) | copy-start | bytes 110596 | tf_op jit(solution)/shard_map/while
  229.1 14.9 %copy-start.16 = (s32[2,9,512]{2,0,1:T(2,128)}, s32[2,9,512]{2,0,1:T(2,128)S(1)}, u32[]{:S(2)}) copy-start(s32[2,9,512]{2,0,1:T(2,128)S(1)} %get-tuple-element.214) | copy-start | bytes 110596 | tf_op jit(solution)/shard_map/while
  293.7 2.8 copy-start
  300.6 3.7 copy-start.11
  300.6 4.6 copy-start.1
  304.3 0.8 copy-start.12
  305.9 5.6 slice-start.2
  306.9 4.5 slice-start.3
  312.0 5.6 slice-start
  313.1 4.5 slice-start.1
  327.2 9.6 %copy-start.8 = (s32[4608]{0:T(1024)S(1)}, s32[4608]{0:T(1024)}, u32[]{:S(2)}) copy-start(s32[4608]{0:T(1024)} %fusion.53) | copy-start | bytes 55300 | tf_op jit(solution)/shard_map/while
  336.8 29.3 %copy-start.17 = (s32[2,9,512]{2,0,1:T(2,128)S(1)}, s32[2,9,512]{2,0,1:T(2,128)}, u32[]{:S(2)}) copy-start(s32[2,9,512]{2,0,1:T(2,128)} %copy-done.16) | copy-start | bytes 110596 | tf_op jit(solution)/shard_map/while
  366.3 5.3 copy-start.13
  367.3 10.7 %collective-permute-start.7 = (f32[128,512]{1,0:T(8,128)}, f32[128,512]{1,0:T(8,128)S(1)}, u32[]{:S(2)}, u32[]{:S(2)}) collective-permute-start(f32[128,512]{1,0:T(8,128)} %get-tuple-element.120), channel_id=1, source_target_pairs={{0,28},{4,0},{8,4},{12,8},{16,12},{20,16},{24,20},{28,24},{1,29},{... | collective-permute-start | bytes 786440 | tf_op jit(solution)/shard_map/ppermute | solution.py:30
  368.0 18.1 %collective-permute-start.9 = (f32[128,512]{1,0:T(8,128)}, f32[128,512]{1,0:T(8,128)}, u32[]{:S(2)}, u32[]{:S(2)}) collective-permute-start(f32[128,512]{1,0:T(8,128)} %get-tuple-element.121), channel_id=1, source_target_pairs={{0,16},{4,20},{8,24},{12,28},{16,0},{20,4},{24,8},{28,12},{1,17},{... | collective-permute-start | bytes 786440 | tf_op jit(solution)/shard_map/ppermute | solution.py:30
  369.3 16.9 %collective-permute-start.8 = (f32[128,512]{1,0:T(8,128)}, f32[128,512]{1,0:T(8,128)}, u32[]{:S(2)}, u32[]{:S(2)}) collective-permute-start(f32[128,512]{1,0:T(8,128)} %get-tuple-element.122), channel_id=1, source_target_pairs={{0,4},{4,8},{8,12},{12,16},{16,20},{20,24},{24,28},{28,0},{1,5},{5... | collective-permute-start | bytes 786440 | tf_op jit(solution)/shard_map/ppermute | solution.py:30
  375.1 14.6 %collective-permute-start.6 = (f32[64,512]{1,0:T(8,128)}, f32[64,512]{1,0:T(8,128)S(1)}, u32[]{:S(2)}, u32[]{:S(2)}) collective-permute-start(f32[64,512]{1,0:T(8,128)} %get-tuple-element.123), channel_id=1, source_target_pairs={{0,3},{1,0},{2,1},{3,2},{4,7},{5,4},{6,5},{7,6},{8,11},{9,8},{10,9... | collective-permute-start | bytes 393224 | tf_op jit(solution)/shard_map/ppermute | solution.py:30
  375.7 12.5 %collective-permute-start.5 = (f32[64,512]{1,0:T(8,128)}, f32[64,512]{1,0:T(8,128)}, u32[]{:S(2)}, u32[]{:S(2)}) collective-permute-start(f32[64,512]{1,0:T(8,128)} %get-tuple-element.124), channel_id=1, source_target_pairs={{0,1},{1,2},{2,3},{3,0},{4,5},{5,6},{6,7},{7,4},{8,9},{9,10},{10,1... | collective-permute-start | bytes 393224 | tf_op jit(solution)/shard_map/ppermute | solution.py:30
  388.1 35.5 %copy-start.20 = (s32[384]{0:T(512)S(1)}, s32[384]{0:T(512)}, u32[]{:S(2)}) copy-start(s32[384]{0:T(512)} %fusion.32) | copy-start | bytes 4612
  427.9 2.8 copy-start.3
  427.9 2.8 copy-start.10
  427.9 2.8 copy-start.14
  430.7 1.6 copy-start.15
  430.7 5.2 copy-start.7
  432.4 145.3 %all-to-all-start.2 = ((f32[4,64,1024]{2,1,0:T(8,128)}), f32[4,64,1024]{2,1,0:T(8,128)S(1)}, u32[]{:S(2)}, u32[]{:S(2)}) async-start(f32[4,64,1024]{2,1,0:T(8,128)} %bitcast.245), calls=%async_computation.2 | async-start | bytes 2097152 | tf_op jit(solution)/shard_map/all_to_all | solution.py:156
  435.9 138.7 %all-reduce.10.cloned.1.call-start = ((), (), s32[]{:S(2)}) async-start(), calls=%async_computation.5 | async-start | bytes 2097152 | tf_op jit(solution)/shard_map/psum | solution.py:149
Sparse Core Ops, SparseCore 0:
  34.7 35.1 all-reduce.5
  388.3 35.3 all-reduce.7
  442.1 132.4 all-reduce.9
where the time goes:
time: 588 us; the launch traced here: 585 us
  waiting for transfers between devices  206 us (35%)
  local copies, waits for them, and re-layouts  196 us (33%)
  other arithmetic  125 us (21%)
  starting transfers between devices  20.8 us (4%)
  blocking collectives  14.8 us (3%)
  between operations  14 us (2%)
  matrix products  8.26 us (1%)
    psum x1, waiting for transfers between devices, local(): total_qkv, total_out = lax.psum((part_qkv, part_out), ('tile', 'head'))  136 us
    scatter-add x2, other arithmetic, attend_block(): totals.at[picks.reshape(-1)]  58.6 us
    while x56, local copies, waits for them, and re-layouts  38.5 us
    gather x2, local copies, waits for them, and re-layouts, attend_block(): near = extended[picks].astype(jnp.float32)  31.2 us
    psum x1, waiting for transfers between devices, local(): backward = lax.psum(jnp.stack(answers), 'head')  30.6 us
    psum x1, waiting for transfers between devices, local(): joined = lax.psum(own_lists.astype(jnp.bfloat16), 'head')  27.8 us
    mul x6, local copies, waits for them, and re-layouts, attend_block(): grad_keys = dscore[..., None] * query_heads[None] * score_scale  21.6 us
    mul x6, local copies, waits for them, and re-layouts, attend_block(): grad_values = probs[..., None] * dout_heads[None]  21.6 us
  transfers between devices with their start and end apart: 16, of which 6 were waited for; matrix products, arithmetic and copies ran while one was open for 6% of the time, Pallas kernels for 0%

commit v1 on v0

v1 whole, which is shorter than its diff:
```python
import functools
import math

import jax
import jax.numpy as jnp
from jax import lax
from jax.experimental import pallas as pl
from jax.experimental.pallas import tpu as pltpu
from jax.sharding import PartitionSpec as P

C = 256
HEADS = 8
NBR = 9
MARGIN = 64
BLOCK = 2 * MARGIN
WINDOW = 2 * BLOCK
NEVER = -1.0e30

NT = (((1,), (1,)), ((), ()))
TN = (((0,), (0,)), ((), ()))


def mm(a, b, dims=(((1,), (0,)), ((), ()))):
    return lax.dot_general(a, b, dims, preferred_element_type=jnp.float32)


def passed_along(value, axis, steps):
    count = lax.axis_size(axis)
    pairs = [(source, (source + steps) % count) for source in range(count)]
    return lax.ppermute(value, axis, pairs)


def attention_body(
    rows, near, keys, grad_scale,
    recv, picks, out,
    q_s, g_s, k_s, kt_s, v_s, vt_s, kw, ktw, vw, vtw, qbd, gbd, p_all, ds_all, gk_s, gv_s, att_s, gq_s,
):
    head_dim = C // HEADS
    scale = 1.0 / math.sqrt(head_dim)
    scale2 = scale / math.log(2.0)
    wide = keys - near + WINDOW
    at_dy = keys
    at_w = keys + rows
    bf16 = jnp.bfloat16

    def weight(t):
        return recv[:, at_w + t * C : at_w + (t + 1) * C]

    q_ext = mm(weight(0), recv[:, :near])
    q_s[...] = pltpu.roll(q_ext, near - MARGIN, 1)[:, :rows].astype(bf16)
    g_s[...] = mm(weight(3), recv[:, at_dy : at_dy + rows]).astype(bf16)
    kt = mm(weight(1), recv[:, :keys])
    kt_s[...] = kt.astype(bf16)
    k_s[...] = kt.T.astype(bf16)
    vt = mm(weight(2), recv[:, :keys])
    vt_s[...] = vt.astype(bf16)
    v_s[...] = vt.T.astype(bf16)
    kw[WINDOW:, :] = k_s[near:, :]
    vw[WINDOW:, :] = v_s[near:, :]
    ktw[:, WINDOW:] = kt_s[:, near:]
    vtw[:, WINDOW:] = vt_s[:, near:]
    qbd[...] = jnp.zeros_like(qbd)
    gbd[...] = jnp.zeros_like(gbd)
    gk_s[...] = jnp.zeros_like(gk_s)
    gv_s[...] = jnp.zeros_like(gv_s)
    gq_s[:, rows:] = jnp.zeros((C, near - rows), jnp.float32)

    def block(b, carry):
        start = pl.multiple_of(b * BLOCK, BLOCK)
        cols = pl.ds(start, BLOCK)
        span = pl.ds(start, WINDOW)
        kw[:WINDOW, :] = k_s[span, :]
        vw[:WINDOW, :] = v_s[span, :]
        ktw[:, :WINDOW] = kt_s[:, span]
        vtw[:, :WINDOW] = vt_s[:, span]
        for h in range(HEADS):
            chan = slice(h * head_dim, (h + 1) * head_dim)
            lane = slice(h * BLOCK, (h + 1) * BLOCK)
            qbd[chan, lane] = q_s[chan, cols]
            gbd[chan, lane] = g_s[chan, cols]
        ids = lax.broadcasted_iota(jnp.int32, (wide, BLOCK), 0)
        count = jnp.zeros((wide, BLOCK), jnp.float32)
        for j in range(NBR):
            count = count + jnp.where(ids == picks[j : j + 1, cols], 1.0, 0.0)
        bias = jnp.where(count > 0.0, jnp.log2(jnp.maximum(count, 1.0)), NEVER)
        bias = jnp.concatenate([bias, bias], axis=1)
        for pair in range(HEADS // 2):
            lane = slice(pair * 2 * BLOCK, (pair + 1) * 2 * BLOCK)
            chan = slice(pair * 2 * head_dim, (pair + 1) * 2 * head_dim)
            low = slice(pair * 2 * head_dim, pair * 2 * head_dim + head_dim)
            high = slice(pair * 2 * head_dim + head_dim, (pair + 1) * 2 * head_dim)
            expon = jnp.exp2(mm(kw[...], qbd[:, lane]) * scale2 + bias)
            total = jnp.sum(expon, axis=0, keepdims=True)
            prob = expon * (1.0 / total)
            dprob = mm(vw[...], gbd[:, lane])
            mean = jnp.sum(prob * dprob, axis=0, keepdims=True)
            dscore = (prob * (dprob - mean)).astype(bf16)
            prob = prob.astype(bf16)
            p_all[:, lane] = prob
            ds_all[:, lane] = dscore
            att = mm(vtw[chan, :], prob).astype(bf16)
            att_s[low, cols] = att[:head_dim, :BLOCK]
            att_s[high, cols] = att[head_dim:, BLOCK:]
            gq = mm(ktw[chan, :], dscore) * scale
            gq_s[low, cols] = gq[:head_dim, :BLOCK]
            gq_s[high, cols] = gq[head_dim:, BLOCK:]
        gk = mm(ds_all[...], qbd[...], NT)
        gk_s[span, :] += gk[:WINDOW]
        gk_s[near:, :] += gk[WINDOW:]
        gv = mm(p_all[...], gbd[...], NT)
        gv_s[span, :] += gv[:WINDOW]
        gv_s[near:, :] += gv[WINDOW:]
        return carry

    lax.fori_loop(0, rows // BLOCK, block, 0)

    gkt = (gk_s[...] * scale).T.astype(bf16)
    gvt = gv_s[...].T.astype(bf16)
    gq = pltpu.roll(gq_s[...], MARGIN, 1).astype(bf16)
    d_all = mm(weight(1), gkt, TN) + mm(weight(2), gvt, TN)
    out[:, :near] = (d_all[:, :near] + mm(weight(0), gq, TN)).astype(bf16)
    out[:, near:keys] = d_all[:, near:].astype(bf16)
    parts = (
        mm(gq, recv[:, :near], NT),
        mm(gkt, recv[:, :keys], NT),
        mm(gvt, recv[:, :keys], NT),
        mm(att_s[...], recv[:, at_dy : at_dy + rows], NT),
    )
    for t, part in enumerate(parts):
        out[:, keys + t * C : keys + (t + 1) * C] = (part * grad_scale).astype(bf16)


def local(tokens, grad_in, w_qkv, w_out, neighbors, send_rows):
    groups = lax.axis_size("tile")
    head_count = lax.axis_size("head")
    border = send_rows.shape[2]
    offsets = (1, groups - 1, groups // 2)
    share, full_rows = tokens.shape
    rows = full_rows // head_count
    near = rows + 2 * MARGIN
    keys = near + 3 * border
    wide = WINDOW + 3 * border
    bf16 = jnp.bfloat16

    flat = send_rows[0].reshape(-1)
    chosen = (lax.broadcasted_iota(jnp.int32, (full_rows, 3 * border), 0) == flat[None, :]).astype(bf16)
    mine = jnp.dot(tokens, chosen, preferred_element_type=jnp.float32).astype(bf16)
    theirs = [
        passed_along(mine[:, p * border : (p + 1) * border], "tile", offsets[p]) for p in range(3)
    ]
    ext = jnp.concatenate([tokens[:, full_rows - MARGIN :], tokens, tokens[:, :MARGIN]], axis=1)
    weights = [w_qkv[0], w_qkv[1], w_qkv[2], w_out]
    sends = jnp.stack(
        [
            jnp.concatenate(
                [ext[:, h * rows : h * rows + near]]
                + theirs
                + [grad_in[:, h * rows : (h + 1) * rows]]
                + weights,
                axis=1,
            )
            for h in range(head_count)
        ]
    )
    recv = lax.all_to_all(sends, "head", split_axis=0, concat_axis=0, tiled=True)
    recv = recv.reshape(C, sends.shape[2])

    start_row = lax.axis_index("head") * rows
    near_ids = lax.dynamic_slice_in_dim(neighbors, start_row, rows, 1)
    block_start = (jnp.arange(rows, dtype=jnp.int32) // BLOCK) * BLOCK
    picks = jnp.where(
        near_ids < full_rows,
        (near_ids - start_row + MARGIN) % full_rows - block_start[None, :],
        near_ids - full_rows + WINDOW,
    )
    grad_scale = 1.0 / math.sqrt(full_rows * groups)
    vm = pltpu.VMEM
    width = keys + 4 * C
    result = pl.pallas_call(
        functools.partial(attention_body, rows, near, keys, grad_scale),
        out_shape=jax.ShapeDtypeStruct((C, width), bf16),
        in_specs=[pl.BlockSpec(memory_space=vm)] * 2,
        out_specs=pl.BlockSpec(memory_space=vm),
        scratch_shapes=[
            vm((C, rows), bf16),
            vm((C, rows), bf16),
            vm((keys, C), bf16),
            vm((C, keys), bf16),
            vm((keys, C), bf16),
            vm((C, keys), bf16),
            vm((wide, C), bf16),
            vm((C, wide), bf16),
            vm((wide, C), bf16),
            vm((C, wide), bf16),
            vm((C, HEADS * BLOCK), bf16),
            vm((C, HEADS * BLOCK), bf16),
            vm((wide, HEADS * BLOCK), bf16),
            vm((wide, HEADS * BLOCK), bf16),
            vm((keys, C), jnp.float32),
            vm((keys, C), jnp.float32),
            vm((C, rows), bf16),
            vm((C, near), jnp.float32),
        ],
        compiler_params=pltpu.CompilerParams(vmem_limit_bytes=56 * 1024 * 1024),
        name="attend",
    )(recv, picks)

    back = lax.all_to_all(
        result.reshape(head_count, share, width), "head", split_axis=0, concat_axis=0, tiled=True
    )
    returned = jnp.sum(back[:, :, near:keys].astype(jnp.float32), axis=0).astype(bf16)
    answers = [
        passed_along(
            returned[:, p * border : (p + 1) * border], "tile", (groups - offsets[p]) % groups
        )
        for p in range(3)
    ]
    partial = jnp.sum(back[:, :, keys:].astype(jnp.float32), axis=0).astype(bf16)
    pieces = lax.all_to_all(
        partial.reshape(groups, -1), "tile", split_axis=0, concat_axis=0, tiled=True
    )
    piece = jnp.sum(pieces.astype(jnp.float32), axis=0).astype(bf16)
    gathered = lax.all_to_all(
        jnp.broadcast_to(piece[None, :], pieces.shape), "tile", split_axis=0, concat_axis=0, tiled=True
    )
    totals = gathered.reshape(share, 4, C).astype(jnp.float32)
    grad_qkv = totals[:, :3].transpose(1, 0, 2)
    grad_out = totals[:, 3]

    gap = jnp.zeros((share, rows - 2 * MARGIN), bf16)
    own = jnp.concatenate([back[h, :, MARGIN : MARGIN + rows] for h in range(head_count)], axis=1)
    edges = jnp.concatenate(
        [
            part
            for h in range(head_count)
            for part in (
                back[(h - 1) % head_count, :, near - MARGIN : near],
                gap,
                back[(h + 1) % head_count, :, :MARGIN],
            )
        ],
        axis=1,
    )
    spread = lax.dot_general(
        jnp.concatenate(answers, axis=1), chosen, NT, preferred_element_type=jnp.float32
    )
    d_tokens = (
        grad_in.astype(jnp.float32) + own.astype(jnp.float32) + edges.astype(jnp.float32) + spread
    )
    return (d_tokens, grad_qkv, grad_out)


def solution(mesh):
    return jax.shard_map(
        local,
        mesh=mesh,
        in_specs=(
            P("head", "tile"),
            P("head", "tile"),
            P(None, "head", None),
            P("head", None),
            P(None, "tile"),
            P("tile", None, None),
        ),
        out_specs=(P("head", "tile"), P(None, "head", None), P("head", None)),
        check_vma=False,
    )
```

time: 588 us -> 128 us (0.22)
  local copies, waits for them, and re-layouts: 196 us -> 6.46 us
  waiting for transfers between devices: 206 us -> 31 us
  other arithmetic: 125 us -> 7.94 us
  Pallas kernels: 0 us -> 31.9 us
  between operations: 14 us -> 0.96 us
  blocking collectives: 14.8 us -> 20.7 us
    psum x3 -> x0, waiting for transfers between devices: 194 us -> none  [the longest x1 136 us: local(): total_qkv, total_out = lax.psum((part_qkv, part_out), ('tile', 'head'))]
    scatter-add x5 -> x0, other arithmetic: 66 us -> none  [the longest x2 58.6 us: attend_block(): totals.at[picks.reshape(-1)]]
    mul x12 -> x0, local copies, waits for them, and re-layouts: 43.2 us -> none  [the longest x6 21.6 us: attend_block(): grad_keys = dscore[..., None] * query_heads[None] * score_scale]
    while x57 -> x0, local copies, waits for them, and re-layouts: 41.1 us -> none
    gather x3 -> x0, local copies, waits for them, and re-layouts: 33.3 us -> none  [the longest x2 31.2 us: attend_block(): near = extended[picks].astype(jnp.float32)]
    pallas_call x0 -> x1, Pallas kernels: none -> 31.9 us  [local(): pl.pallas_call(functools.partial(attention_body, rows, near, keys, grad_s...]
    all_to_all x3, waiting for transfers between devices: 0.01 us -> 27.6 us  [the longest x1 21.3 us: local(): lax.all_to_all(sends, 'head', split_axis=0, concat_axis=0, tiled=True)]
    concatenate x5 -> x2, local copies, waits for them, and re-layouts: 23.9 us -> 0.52 us  [the longest x1 0.51 us: local(): jnp.concatenate([part for h in range(head_count) for part in (back[(h - 1...]
  transfers between devices with their start and end apart: 16 -> 9, of which waited for: 6 -> 5; matrix products, arithmetic and copies ran while one was open for 6% -> 6% of each run, Pallas kernels for 0% -> 0%
where the time goes in v1:
time: 128 us
  Pallas kernels  31.9 us (25%)
  waiting for transfers between devices  31 us (24%)
  starting transfers between devices  24 us (19%)
  blocking collectives  20.7 us (16%)
  other arithmetic  7.94 us (6%)
  local copies, waits for them, and re-layouts  6.46 us (5%)
  matrix products  4.8 us (4%)
    pallas_call x1, Pallas kernels, local(): pl.pallas_call(functools.partial(attention_body, rows, near, keys, grad_s...  31.9 us
    all_to_all x1, waiting for transfers between devices, local(): lax.all_to_all(sends, 'head', split_axis=0, concat_axis=0, tiled=True)  21.3 us
    all_to_all x1, blocking collectives, local(): lax.all_to_all(result.reshape(head_count, share, width), 'head', split_ax...  20.7 us
    ppermute x6, starting transfers between devices, passed_along(): return lax.ppermute(value, axis, pairs)  12 us
    all_to_all x1, starting transfers between devices, local(): lax.all_to_all(jnp.broadcast_to(piece[None, :], pieces.shape), 'tile', sp...  5.1 us
    all_to_all x1, waiting for transfers between devices, local(): lax.all_to_all(jnp.broadcast_to(piece[None, :], pieces.shape), 'tile', sp...  4.88 us
    unnamed x26, local copies, waits for them, and re-layouts  4.49 us
    all_to_all x1, starting transfers between devices, local(): lax.all_to_all(sends, 'head', split_axis=0, concat_axis=0, tiled=True)  3.58 us
  transfers between devices with their start and end apart: 9, of which 5 were waited for; matrix products, arithmetic and copies ran while one was open for 6% of the time, Pallas kernels for 0%

profile of v1, /device:TPU:0, one launch (start us, length us, event | category | flops | bytes accessed | tf_op | source)
XLA Modules:
  0.0 127.7 jit_solution(12180860291075893855)
XLA Ops:
  0.6 0.0 copy-start.1
  0.6 0.8 reduce.4
  1.4 0.0 copy-start.3
  1.4 2.4 %fusion.6 = bf16[64,384]{1,0:T(8,128)(2,1)S(1)} fusion(bf16[64,4096]{1,0:T(8,128)(2,1)} %param.6, s32[384]{0:T(512)S(1)} %bitcast.61), kind=kOutput, calls=%fused_computation.8 | convolution fusion | flops 202924032 | bytes 574976 | tf_op jit(solution)/shard_map/dot_general | solution.py:147
  3.8 0.0 copy-start.2
  3.8 0.0 copy-start.4
  3.8 3.0 %collective-permute-start = (bf16[64,128]{1,0:T(8,128)(2,1)S(1)}, bf16[64,128]{1,0:T(8,128)(2,1)S(1)}, u32[]{:S(2)}, u32[]{:S(2)}) collective-permute-start(bf16[64,128]{1,0:T(8,128)(2,1)S(1)} %get-tuple-element.48), channel_id=1, source_target_pairs={{0,4},{4,8},{8,12},{12,16},{16,20},{20,24},{24,28},{28,0},{1,5},{5... | collective-permute-start | bytes 49160 | tf_op jit(solution)/shard_map/ppermute | solution.py:30
  6.9 3.1 %collective-permute-start.1 = (bf16[64,128]{1,0:T(8,128)(2,1)S(1)}, bf16[64,128]{1,0:T(8,128)(2,1)S(1)}, u32[]{:S(2)}, u32[]{:S(2)}) collective-permute-start(bf16[64,128]{1,0:T(8,128)(2,1)S(1)} %get-tuple-element.47), channel_id=1, source_target_pairs={{0,28},{4,0},{8,4},{12,8},{16,12},{20,16},{24,20},{28,24},{1,29},{... | collective-permute-start | bytes 49160 | tf_op jit(solution)/shard_map/ppermute | solution.py:30
  10.0 0.9 collective-permute-start.2
  10.9 0.0 copy-done.1
  10.9 0.1 fusion.22
  10.9 0.3 fusion.8
  11.2 0.4 collective-permute-done
  11.6 0.0 collective-permute-done.1
  11.7 2.9 %collective-permute-done.2 = bf16[64,128]{1,0:T(8,128)(2,1)S(1)} collective-permute-done((bf16[64,128]{1,0:T(8,128)(2,1)S(1)}, bf16[64,128]{1,0:T(8,128)(2,1)S(1)}, u32[]{:S(2)}, u32[]{:S(2)}) %collective-permute-start.2) | collective-permute-done | bytes 16416 | tf_op jit(solution)/shard_map/ppermute | solution.py:30
  14.6 0.0 copy-done.3
  14.7 0.0 copy-done.2
  14.8 0.0 copy-done.4
  14.8 1.5 %pad_maximum_fusion = bf16[4,64,3584]{2,1,0:T(8,128)(2,1)} fusion(bf16[1,64,3584]{2,1,0:T(8,128)(2,1)S(1)} %bitcast.59, bf16[1,64,3584]{2,1,0:T(8,128)(2,1)S(1)} %bitcast.57, bf16[1,64,3584]{2,1,0:T(8,128)(2,1)S(1)} %bitcast.58, bf16[1,64,3584]{2,1,0:T(8,128)(2,1)S(1)} %bitcast.56), kind=kLoop, calls=%fused_computation.6 | loop fusion | flops 2752512 | bytes 3670016 | tf_op jit(solution)/shard_map/stack | solution.py:153
  16.3 3.6 %all-to-all-start = ((bf16[4,64,3584]{2,1,0:T(8,128)(2,1)}), bf16[4,64,3584]{2,1,0:T(8,128)(2,1)S(1)}, u32[]{:S(2)}, u32[]{:S(2)}) async-start(bf16[4,64,3584]{2,1,0:T(8,128)(2,1)} %pad_maximum_fusion), calls=%async_computation | async-start | bytes 3670016 | tf_op jit(solution)/shard_map/all_to_all | solution.py:165
  19.9 1.5 %fusion.11.picks = s32[9,1024]{1,0:T(8,128)} fusion(s32[9,4096]{1,0:T(8,128)} %param.10, s32[]{:T(128)S(6)} %select_n.23, s32[1024]{0:T(1024)S(1)} %fusion.17, s32[]{:T(128)S(6)} %mul.11), kind=kLoop, calls=%fused_computation.60 | loop fusion | flops 156672 | bytes 77832 | tf_op jit(solution)/shard_map/jit(_where)/select_n | solution.py:171
  21.4 21.3 %all-to-all-done = bf16[4,64,3584]{2,1,0:T(8,128)(2,1)S(1)} async-done(((bf16[4,64,3584]{2,1,0:T(8,128)(2,1)}), bf16[4,64,3584]{2,1,0:T(8,128)(2,1)S(1)}, u32[]{:S(2)}, u32[]{:S(2)}) %all-to-all-start) | async-done | bytes 1835040 | tf_op jit(solution)/shard_map/all_to_all | solution.py:165
  42.7 0.0 copy-start
  42.7 1.3 copy-done
  44.0 31.9 %attend.1 = bf16[256,2560]{1,0:T(8,128)(2,1)} custom-call(bf16[256,3584]{1,0:T(8,128)(2,1)} %bitcast.54, s32[9,1024]{1,0:T(8,128)} %fusion.11.picks), custom_call_target="tpu_custom_call" | custom-call | tf_op jit(solution)/shard_map/attend/pallas_call | solution.py:179
  75.8 20.7 %all_to_all.26 = bf16[4,64,2560]{2,1,0:T(8,128)(2,1)S(1)} all-to-all(bf16[4,64,2560]{2,1,0:T(8,128)(2,1)} %bitcast.55), channel_id=1, replica_groups=mesh['tile'=8,'head'=4] {'head'}, dimensions={0} | all-to-all | bytes 2621440 | tf_op jit(solution)/shard_map/all_to_all | solution.py:208
  96.6 0.1 slice_reduce_fusion
  96.7 0.1 all_to_all.21
  96.8 0.5 broadcast.53
  97.3 1.4 %reduce.7 = bf16[8,8192]{1,0:T(8,128)(2,1)S(1)} reduce(bf16[8,1,8192]{2,1,0:T(2,128)(2,1)S(1)} %all_to_all.21, bf16[]{:T(256)} %broadcast.53), dimensions={1}, to_apply=%all_to_all.21.reduce_sub_computation | reduce | bytes 262146 | tf_op jit(solution)/shard_map/all_to_all | solution.py:219
  98.7 0.7 reshape.46
  99.4 3.4 %all-to-all-start.2 = ((bf16[8,2,4096]{2,1,0:T(2,128)(2,1)}), bf16[8,2,4096]{2,1,0:T(2,128)(2,1)S(1)}, u32[]{:S(2)}, u32[]{:S(2)}) async-start(bf16[8,2,4096]{2,1,0:T(2,128)(2,1)} %reshape.46), calls=%async_computation.2 | async-start | bytes 262144 | tf_op jit(solution)/shard_map/all_to_all | solution.py:219
  102.9 4.7 %collective-permute-start.3 = (bf16[64,128]{1,0:T(8,128)(2,1)S(1)}, bf16[64,128]{1,0:T(8,128)(2,1)S(1)}, u32[]{:S(2)}, u32[]{:S(2)}) collective-permute-start(bf16[64,128]{1,0:T(8,128)(2,1)S(1)} %get-tuple-element.43), channel_id=1, source_target_pairs={{0,28},{4,0},{8,4},{12,8},{16,12},{20,16},{24,20},{28,24},{1,29},{... | collective-permute-start | bytes 49160 | tf_op jit(solution)/shard_map/ppermute | solution.py:30
  107.6 0.0 collective-permute-start.4
  107.6 0.2 collective-permute-start.5
  107.8 0.2 slice_bitcast_fusion.4
  108.0 0.1 slice_bitcast_fusion.5
  108.1 0.5 concatenate.35
  108.6 1.4 %all-to-all-done.2 = bf16[8,2,4096]{2,1,0:T(2,128)(2,1)S(1)} async-done(((bf16[8,2,4096]{2,1,0:T(2,128)(2,1)}), bf16[8,2,4096]{2,1,0:T(2,128)(2,1)S(1)}, u32[]{:S(2)}, u32[]{:S(2)}) %all-to-all-start.2) | async-done | bytes 131104 | tf_op jit(solution)/shard_map/all_to_all | solution.py:219
  110.1 0.1 reshape.47
  110.2 0.3 reduce_sum.38
  110.5 0.1 broadcast_in_dim.5
  110.6 1.4 %reduce.8 = bf16[8,8192]{1,0:T(8,128)(2,1)S(1)} reduce(bf16[8,1,8192]{2,1,0:T(2,128)(2,1)S(1)} %broadcast_in_dim.5, bf16[]{:T(256)} %broadcast.53), dimensions={1}, to_apply=%broadcast_in_dim.5.reduce_sub_computation | reduce | bytes 262146 | tf_op jit(solution)/shard_map/broadcast_in_dim | solution.py:224
  112.1 0.7 reshape.48
  112.8 5.1 %all-to-all-start.3 = ((bf16[8,2,4096]{2,1,0:T(2,128)(2,1)}), bf16[8,2,4096]{2,1,0:T(2,128)(2,1)S(1)}, u32[]{:S(2)}, u32[]{:S(2)}) async-start(bf16[8,2,4096]{2,1,0:T(2,128)(2,1)} %reshape.48), calls=%async_computation.3 | async-start | bytes 262144 | tf_op jit(solution)/shard_map/all_to_all | solution.py:223
  117.9 0.0 collective-permute-done.3
  117.9 0.0 collective-permute-done.4
  117.9 0.0 collective-permute-done.5
  117.9 2.4 %fusion.2 = f32[64,4096]{1,0:T(8,128)} fusion(s32[384]{0:T(512)S(1)} %bitcast.62, bf16[64,4096]{1,0:T(8,128)(2,1)S(1)} %concatenate.35, bf16[64,4096]{1,0:T(8,128)(2,1)S(1)} %copy-done.3, bf16[64,1024]{1,0:T(8,128)(2,1)S(1)} %get-tuple-element.13, bf16[64,1024]{1,0:T(8,128)(2,1)S(1)} %get-tuple-element.14, bf16[64,1024]{1,0:T(8,128)(2,1)S(1)} %get-tuple-element.15, ...), kind=kOutput, calls=%fused_computation.3 | convolution fusion | flops 206454784 | bytes 2672128 | tf_op jit(solution)/shard_map/dot_general | solution.py:244
  120.4 4.9 %all-to-all-done.3 = bf16[8,2,4096]{2,1,0:T(2,128)(2,1)S(1)} async-done(((bf16[8,2,4096]{2,1,0:T(2,128)(2,1)}), bf16[8,2,4096]{2,1,0:T(2,128)(2,1)S(1)}, u32[]{:S(2)}, u32[]{:S(2)}) %all-to-all-start.3) | async-done | bytes 131104 | tf_op jit(solution)/shard_map/all_to_all | solution.py:223
  125.2 0.1 reshape.49
  125.4 0.7 convert_reduce_fusion
  126.1 0.2 reshape.43
  126.3 0.1 slice.163
  126.4 0.7 copy.12
  127.1 0.6 copy.15
  (17 shorter events, 0.3 us)
Async XLA Ops:
  0.6 10.2 %copy-start.1 = (bf16[64,4096]{1,0:T(8,128)(2,1)S(1)}, bf16[64,4096]{1,0:T(8,128)(2,1)}, u32[]{:S(2)}) copy-start(bf16[64,4096]{1,0:T(8,128)(2,1)} %param.6) | copy-start | bytes 1572868
  1.4 13.2 %copy-start.3 = (bf16[64,4096]{1,0:T(8,128)(2,1)S(1)}, bf16[64,4096]{1,0:T(8,128)(2,1)}, u32[]{:S(2)}) copy-start(bf16[64,4096]{1,0:T(8,128)(2,1)} %param.7) | copy-start | bytes 1572868
  3.8 10.9 %copy-start.2 = (bf16[3,64,256]{2,1,0:T(8,128)(2,1)S(1)}, bf16[3,64,256]{2,1,0:T(8,128)(2,1)}, u32[]{:S(2)}) copy-start(bf16[3,64,256]{2,1,0:T(8,128)(2,1)} %param.8) | copy-start | bytes 294916
  3.8 11.0 %copy-start.4 = (bf16[64,256]{1,0:T(8,128)(2,1)S(1)}, bf16[64,256]{1,0:T(8,128)(2,1)}, u32[]{:S(2)}) copy-start(bf16[64,256]{1,0:T(8,128)(2,1)} %param.9) | copy-start | bytes 98308
  3.8 7.8 %collective-permute-start = (bf16[64,128]{1,0:T(8,128)(2,1)S(1)}, bf16[64,128]{1,0:T(8,128)(2,1)S(1)}, u32[]{:S(2)}, u32[]{:S(2)}) collective-permute-start(bf16[64,128]{1,0:T(8,128)(2,1)S(1)} %get-tuple-element.48), channel_id=1, source_target_pairs={{0,4},{4,8},{8,12},{12,16},{16,20},{20,24},{24,28},{28,0},{1,5},{5... | collective-permute-start | bytes 49160 | tf_op jit(solution)/shard_map/ppermute | solution.py:30
  6.9 4.8 %collective-permute-start.1 = (bf16[64,128]{1,0:T(8,128)(2,1)S(1)}, bf16[64,128]{1,0:T(8,128)(2,1)S(1)}, u32[]{:S(2)}, u32[]{:S(2)}) collective-permute-start(bf16[64,128]{1,0:T(8,128)(2,1)S(1)} %get-tuple-element.47), channel_id=1, source_target_pairs={{0,28},{4,0},{8,4},{12,8},{16,12},{20,16},{24,20},{28,24},{1,29},{... | collective-permute-start | bytes 49160 | tf_op jit(solution)/shard_map/ppermute | solution.py:30
  10.0 4.6 %collective-permute-start.2 = (bf16[64,128]{1,0:T(8,128)(2,1)S(1)}, bf16[64,128]{1,0:T(8,128)(2,1)S(1)}, u32[]{:S(2)}, u32[]{:S(2)}) collective-permute-start(bf16[64,128]{1,0:T(8,128)(2,1)S(1)} %get-tuple-element.46), channel_id=1, source_target_pairs={{0,16},{4,20},{8,24},{12,28},{16,0},{20,4},{24,8},{28,12},{1,17},{... | collective-permute-start | bytes 49160 | tf_op jit(solution)/shard_map/ppermute | solution.py:30
  16.3 26.4 %all-to-all-start = ((bf16[4,64,3584]{2,1,0:T(8,128)(2,1)}), bf16[4,64,3584]{2,1,0:T(8,128)(2,1)S(1)}, u32[]{:S(2)}, u32[]{:S(2)}) async-start(bf16[4,64,3584]{2,1,0:T(8,128)(2,1)} %pad_maximum_fusion), calls=%async_computation | async-start | bytes 3670016 | tf_op jit(solution)/shard_map/all_to_all | solution.py:165
  42.7 1.3 copy-start
  99.4 10.7 %all-to-all-start.2 = ((bf16[8,2,4096]{2,1,0:T(2,128)(2,1)}), bf16[8,2,4096]{2,1,0:T(2,128)(2,1)S(1)}, u32[]{:S(2)}, u32[]{:S(2)}) async-start(bf16[8,2,4096]{2,1,0:T(2,128)(2,1)} %reshape.46), calls=%async_computation.2 | async-start | bytes 262144 | tf_op jit(solution)/shard_map/all_to_all | solution.py:219
  102.9 15.0 %collective-permute-start.3 = (bf16[64,128]{1,0:T(8,128)(2,1)S(1)}, bf16[64,128]{1,0:T(8,128)(2,1)S(1)}, u32[]{:S(2)}, u32[]{:S(2)}) collective-permute-start(bf16[64,128]{1,0:T(8,128)(2,1)S(1)} %get-tuple-element.43), channel_id=1, source_target_pairs={{0,28},{4,0},{8,4},{12,8},{16,12},{20,16},{24,20},{28,24},{1,29},{... | collective-permute-start | bytes 49160 | tf_op jit(solution)/shard_map/ppermute | solution.py:30
  107.6 10.3 %collective-permute-start.4 = (bf16[64,128]{1,0:T(8,128)(2,1)S(1)}, bf16[64,128]{1,0:T(8,128)(2,1)S(1)}, u32[]{:S(2)}, u32[]{:S(2)}) collective-permute-start(bf16[64,128]{1,0:T(8,128)(2,1)S(1)} %get-tuple-element.45), channel_id=1, source_target_pairs={{0,4},{4,8},{8,12},{12,16},{16,20},{20,24},{24,28},{28,0},{1,5},{5... | collective-permute-start | bytes 49160 | tf_op jit(solution)/shard_map/ppermute | solution.py:30
  107.6 10.3 %collective-permute-start.5 = (bf16[64,128]{1,0:T(8,128)(2,1)S(1)}, bf16[64,128]{1,0:T(8,128)(2,1)S(1)}, u32[]{:S(2)}, u32[]{:S(2)}) collective-permute-start(bf16[64,128]{1,0:T(8,128)(2,1)S(1)} %get-tuple-element.44), channel_id=1, source_target_pairs={{0,16},{4,20},{8,24},{12,28},{16,0},{20,4},{24,8},{28,12},{1,17},{... | collective-permute-start | bytes 49160 | tf_op jit(solution)/shard_map/ppermute | solution.py:30
  112.8 12.4 %all-to-all-start.3 = ((bf16[8,2,4096]{2,1,0:T(2,128)(2,1)}), bf16[8,2,4096]{2,1,0:T(2,128)(2,1)S(1)}, u32[]{:S(2)}, u32[]{:S(2)}) async-start(bf16[8,2,4096]{2,1,0:T(2,128)(2,1)} %reshape.48), calls=%async_computation.3 | async-start | bytes 262144 | tf_op jit(solution)/shard_map/all_to_all | solution.py:223

commit v2 on v1

--- a/solution.py
+++ b/solution.py
@@ -22,12 +22,6 @@
 
 def mm(a, b, dims=(((1,), (0,)), ((), ()))):
     return lax.dot_general(a, b, dims, preferred_element_type=jnp.float32)
-
-
-def passed_along(value, axis, steps):
-    count = lax.axis_size(axis)
-    pairs = [(source, (source + steps) % count) for source in range(count)]
-    return lax.ppermute(value, axis, pairs)
 
 
 def attention_body(
@@ -39,20 +33,20 @@
     scale = 1.0 / math.sqrt(head_dim)
     scale2 = scale / math.log(2.0)
     wide = keys - near + WINDOW
-    at_dy = keys
-    at_w = keys + rows
+    at_x = rows
+    at_w = rows + keys
     bf16 = jnp.bfloat16
 
     def weight(t):
         return recv[:, at_w + t * C : at_w + (t + 1) * C]
 
-    q_ext = mm(weight(0), recv[:, :near])
+    q_ext = mm(weight(0), recv[:, at_x : at_x + near])
     q_s[...] = pltpu.roll(q_ext, near - MARGIN, 1)[:, :rows].astype(bf16)
-    g_s[...] = mm(weight(3), recv[:, at_dy : at_dy + rows]).astype(bf16)
-    kt = mm(weight(1), recv[:, :keys])
+    g_s[...] = mm(weight(3), recv[:, :rows]).astype(bf16)
+    kt = mm(weight(1), recv[:, at_x : at_x + keys])
     kt_s[...] = kt.astype(bf16)
     k_s[...] = kt.T.astype(bf16)
-    vt = mm(weight(2), recv[:, :keys])
+    vt = mm(weight(2), recv[:, at_x : at_x + keys])
     vt_s[...] = vt.astype(bf16)
     v_s[...] = vt.T.astype(bf16)
     kw[WINDOW:, :] = k_s[near:, :]
@@ -121,13 +115,166 @@
     out[:, :near] = (d_all[:, :near] + mm(weight(0), gq, TN)).astype(bf16)
     out[:, near:keys] = d_all[:, near:].astype(bf16)
     parts = (
-        mm(gq, recv[:, :near], NT),
-        mm(gkt, recv[:, :keys], NT),
-        mm(gvt, recv[:, :keys], NT),
-        mm(att_s[...], recv[:, at_dy : at_dy + rows], NT),
+        mm(gq, recv[:, at_x : at_x + near], NT),
+        mm(gkt, recv[:, at_x : at_x + keys], NT),
+        mm(gvt, recv[:, at_x : at_x + keys], NT),
+        mm(att_s[...], recv[:, :rows], NT),
     )
     for t, part in enumerate(parts):
         out[:, keys + t * C : keys + (t + 1) * C] = (part * grad_scale).astype(bf16)
+
+
+def on_mesh(tile, head):
+    return {"tile": tile, "head": head}
+
+
+def greet(peers):
+    barrier = pltpu.get_barrier_semaphore()
+    for peer in peers:
+        pl.semaphore_signal(barrier, inc=1, device_id=peer, device_id_type=pl.DeviceIdType.MESH)
+    pl.semaphore_wait(barrier, len(peers))
+
+
+def send(src, dst, send_sem, recv_sem, peer):
+    copy = pltpu.make_async_remote_copy(
+        src_ref=src,
+        dst_ref=dst,
+        send_sem=send_sem,
+        recv_sem=recv_sem,
+        device_id=peer,
+        device_id_type=pl.DeviceIdType.MESH,
+    )
+    copy.start()
+    return copy
+
+
+def exchange_in(
+    groups, heads, share, border, body, keys, pieces, mine, w, recv,
+    halo, w_send, w_recv, wf_send, wf_recv, p_send, p_recv, b_send, b_recv, bf_send, bf_recv, l_send, l_recv,
+):
+    tile, me = lax.axis_index("tile"), lax.axis_index("head")
+    offsets = (1, groups - 1, groups // 2)
+    partner = (me // 2) * 2 + 1 - me % 2
+    at_b, at_w = body, body + 3 * border
+    full = recv.shape[1]
+
+    def rows_of(index):
+        return pl.ds(pl.multiple_of(index * share, share), share)
+
+    greet(
+        [on_mesh(tile, (me + k) % heads) for k in range(1, heads)]
+        + [on_mesh((tile + step) % groups, me) for step in offsets]
+    )
+    lists = [
+        send(mine.at[p], halo.at[p], l_send.at[p], l_recv.at[p], on_mesh((tile + offsets[p]) % groups, me))
+        for p in range(3)
+    ]
+    steps = range(2, heads, 2)
+    w_here = recv.at[rows_of(me), at_w:full]
+    w_copies = [
+        send(w, w_here, w_send.at[i], w_recv.at[i], on_mesh(tile, (me + k) % heads))
+        for i, k in enumerate(steps)
+    ]
+    w_near = send(w, w_here, w_send.at[len(steps)], w_recv.at[len(steps)], on_mesh(tile, partner))
+    sends = []
+    for k in range(1, heads):
+        to = (me + k) % heads
+        sends.append(
+            send(pieces.at[to], recv.at[rows_of(me), 0:body], p_send.at[k - 1], p_recv.at[k - 1], on_mesh(tile, to))
+        )
+    recv[rows_of(me), 0:body] = pieces[me]
+    recv[rows_of(me), at_w:full] = w[...]
+    for copy in lists:
+        copy.wait()
+    b_copies = []
+    for p in range(3):
+        cols = slice(at_b + p * border, at_b + (p + 1) * border)
+        for i, k in enumerate(steps):
+            b_copies.append(
+                send(halo.at[p], recv.at[rows_of(me), cols], b_send.at[p, i], b_recv.at[p, i], on_mesh(tile, (me + k) % heads))
+            )
+        b_copies.append(
+            send(halo.at[p], recv.at[rows_of(me), cols], b_send.at[p, len(steps)], b_recv.at[p, len(steps)], on_mesh(tile, partner))
+        )
+        recv[rows_of(me), cols] = halo[p]
+    last = []
+    for i, k in enumerate(steps):
+        w_copies[i].wait()
+        block = recv.at[rows_of((me + heads - k) % heads), at_w:full]
+        last.append(send(block, block, wf_send.at[i], wf_recv.at[i], on_mesh(tile, partner)))
+    w_near.wait()
+    for copy in b_copies:
+        copy.wait()
+    for i, k in enumerate(steps):
+        block = recv.at[rows_of((me + heads - k) % heads), at_b:at_w]
+        last.append(send(block, block, bf_send.at[i], bf_recv.at[i], on_mesh(tile, partner)))
+    for copy in sends + last:
+        copy.wait()
+
+
+def exchange_out(
+    groups, heads, share, border, near, keys, result, own, answers, totals,
+    dwr, br, s1, rs, ansb, w_send, w_recv, b_send, b_recv, d_send, d_recv, r_send, r_recv, g_send, g_recv, a_send, a_recv,
+):
+    tile, me = lax.axis_index("tile"), lax.axis_index("head")
+    offsets = (1, groups - 1, groups // 2)
+    full = result.shape[1]
+    depth = s1.shape[1]
+    blocks = (full - keys) // 128
+
+    def rows_of(index):
+        return pl.ds(pl.multiple_of(index * share, share), share)
+
+    others = [(me + k) % heads for k in range(1, heads)]
+    peers = [(tile + k) % groups for k in range(1, groups)]
+    greet([on_mesh(tile, to) for to in others] + [on_mesh(to, me) for to in peers])
+    w_copies = [
+        send(result.at[rows_of(to), keys:full], dwr.at[i], w_send.at[i], w_recv.at[i], on_mesh(tile, to))
+        for i, to in enumerate(others)
+    ]
+    b_copies = [
+        send(result.at[rows_of(to), near:keys], br.at[i], b_send.at[i], b_recv.at[i], on_mesh(tile, to))
+        for i, to in enumerate(others)
+    ]
+    d_copies = [
+        send(result.at[rows_of(to), 0:near], own.at[me], d_send.at[i], d_recv.at[i], on_mesh(tile, to))
+        for i, to in enumerate(others)
+    ]
+    own[me] = result[rows_of(me), 0:near]
+    for copy in w_copies:
+        copy.wait()
+    total = result[rows_of(me), keys:full].astype(jnp.float32)
+    for i in range(heads - 1):
+        total = total + dwr[i].astype(jnp.float32)
+    for g in range(groups):
+        row, col = (g // blocks) * depth, (g % blocks) * 128
+        s1[g] = total[row : row + depth, col : col + 128].astype(jnp.bfloat16)
+    r_copies = [
+        send(s1.at[to], rs.at[i], r_send.at[i], r_recv.at[i], on_mesh(to, me)) for i, to in enumerate(peers)
+    ]
+    for copy in b_copies:
+        copy.wait()
+    back = result[rows_of(me), near:keys].astype(jnp.float32)
+    for i in range(heads - 1):
+        back = back + br[i].astype(jnp.float32)
+    for p in range(3):
+        ansb[p] = back[:, p * border : (p + 1) * border].astype(jnp.bfloat16)
+    a_copies = [
+        send(ansb.at[p], answers.at[p], a_send.at[p], a_recv.at[p], on_mesh((tile + groups - offsets[p]) % groups, me))
+        for p in range(3)
+    ]
+    for copy in r_copies:
+        copy.wait()
+    piece = s1[tile].astype(jnp.float32)
+    for i in range(groups - 1):
+        piece = piece + rs[i].astype(jnp.float32)
+    totals[tile] = piece.astype(jnp.bfloat16)
+    g_copies = [
+        send(totals.at[tile], totals.at[tile], g_send.at[i], g_recv.at[i], on_mesh(to, me))
+        for i, to in enumerate(peers)
+    ]
+    for copy in a_copies + g_copies + d_copies:
+        copy.wait()
 
 
 def local(tokens, grad_in, w_qkv, w_out, neighbors, send_rows):
@@ -145,25 +292,37 @@
     flat = send_rows[0].reshape(-1)
     chosen = (lax.broadcasted_iota(jnp.int32, (full_rows, 3 * border), 0) == flat[None, :]).astype(bf16)
     mine = jnp.dot(tokens, chosen, preferred_element_type=jnp.float32).astype(bf16)
-    theirs = [
-        passed_along(mine[:, p * border : (p + 1) * border], "tile", offsets[p]) for p in range(3)
-    ]
+    mine = mine.reshape(share, 3, border).transpose(1, 0, 2)
     ext = jnp.concatenate([tokens[:, full_rows - MARGIN :], tokens, tokens[:, :MARGIN]], axis=1)
-    weights = [w_qkv[0], w_qkv[1], w_qkv[2], w_out]
+    weights = jnp.concatenate([w_qkv[0], w_qkv[1], w_qkv[2], w_out], axis=1)
     sends = jnp.stack(
         [
             jnp.concatenate(
-                [ext[:, h * rows : h * rows + near]]
-                + theirs
-                + [grad_in[:, h * rows : (h + 1) * rows]]
-                + weights,
-                axis=1,
+                [grad_in[:, h * rows : (h + 1) * rows], ext[:, h * rows : h * rows + near]], axis=1
             )
             for h in range(head_count)
         ]
     )
-    recv = lax.all_to_all(sends, "head", split_axis=0, concat_axis=0, tiled=True)
-    recv = recv.reshape(C, sends.shape[2])
+    vm = pltpu.VMEM
+    dma = pltpu.SemaphoreType.DMA
+    far = (head_count - 1) // 2
+    recv = pl.pallas_call(
+        functools.partial(exchange_in, groups, head_count, share, border, rows + near, keys),
+        out_shape=jax.ShapeDtypeStruct((C, rows + keys + 4 * C), bf16),
+        in_specs=[pl.BlockSpec(memory_space=vm)] * 3,
+        out_specs=pl.BlockSpec(memory_space=vm),
+        scratch_shapes=[
+            vm((3, share, border), bf16),
+            dma((far + 1,)), dma((far + 1,)), dma((far,)), dma((far,)),
+            dma((head_count - 1,)), dma((head_count - 1,)),
+            dma((3, far + 1)), dma((3, far + 1)), dma((far,)), dma((far,)),
+            dma((3,)), dma((3,)),
+        ],
+        compiler_params=pltpu.CompilerParams(
+            collective_id=0, has_side_effects=True, vmem_limit_bytes=24 * 1024 * 1024
+        ),
+        name="exchange_in",
+    )(sends, mine, weights)
 
     start_row = lax.axis_index("head") * rows
     near_ids = lax.dynamic_slice_in_dim(neighbors, start_row, rows, 1)
@@ -174,7 +333,6 @@
         near_ids - full_rows + WINDOW,
     )
     grad_scale = 1.0 / math.sqrt(full_rows * groups)
-    vm = pltpu.VMEM
     width = keys + 4 * C
     result = pl.pallas_call(
         functools.partial(attention_body, rows, near, keys, grad_scale),
@@ -205,25 +363,35 @@
         name="attend",
     )(recv, picks)
 
-    back = lax.all_to_all(
-        result.reshape(head_count, share, width), "head", split_axis=0, concat_axis=0, tiled=True
-    )
-    returned = jnp.sum(back[:, :, near:keys].astype(jnp.float32), axis=0).astype(bf16)
-    answers = [
-        passed_along(
-            returned[:, p * border : (p + 1) * border], "tile", (groups - offsets[p]) % groups
-        )
-        for p in range(3)
-    ]
-    partial = jnp.sum(back[:, :, keys:].astype(jnp.float32), axis=0).astype(bf16)
-    pieces = lax.all_to_all(
-        partial.reshape(groups, -1), "tile", split_axis=0, concat_axis=0, tiled=True
-    )
-    piece = jnp.sum(pieces.astype(jnp.float32), axis=0).astype(bf16)
-    gathered = lax.all_to_all(
-        jnp.broadcast_to(piece[None, :], pieces.shape), "tile", split_axis=0, concat_axis=0, tiled=True
-    )
-    totals = gathered.reshape(share, 4, C).astype(jnp.float32)
+    depth = share * 4 * C // 128 // groups
+    others, peers = head_count - 1, groups - 1
+    back, answers, totals = pl.pallas_call(
+        functools.partial(exchange_out, groups, head_count, share, border, near, keys),
+        out_shape=(
+            jax.ShapeDtypeStruct((head_count, share, near), bf16),
+            jax.ShapeDtypeStruct((3, share, border), bf16),
+            jax.ShapeDtypeStruct((groups, depth, 128), bf16),
+        ),
+        in_specs=[pl.BlockSpec(memory_space=vm)],
+        out_specs=[pl.BlockSpec(memory_space=vm)] * 3,
+        scratch_shapes=[
+            vm((others, share, 4 * C), bf16),
+            vm((others, share, 3 * border), bf16),
+            vm((groups, depth, 128), bf16),
+            vm((peers, depth, 128), bf16),
+            vm((3, share, border), bf16),
+        ]
+        + [dma((others,))] * 6
+        + [dma((peers,))] * 4
+        + [dma((3,))] * 2,
+        compiler_params=pltpu.CompilerParams(
+            collective_id=1, has_side_effects=True, vmem_limit_bytes=24 * 1024 * 1024
+        ),
+        name="exchange_out",
+    )(result)
+    blocks = 4 * C // 128
+    totals = totals.reshape(groups // blocks, blocks, depth, 128).transpose(0, 2, 1, 3)
+    totals = totals.reshape(share, 4, C).astype(jnp.float32)
     grad_qkv = totals[:, :3].transpose(1, 0, 2)
     grad_out = totals[:, 3]
 
@@ -242,7 +410,7 @@
         axis=1,
     )
     spread = lax.dot_general(
-        jnp.concatenate(answers, axis=1), chosen, NT, preferred_element_type=jnp.float32
+        answers.transpose(1, 0, 2).reshape(share, 3 * border), chosen, NT, preferred_element_type=jnp.float32
     )
     d_tokens = (
         grad_in.astype(jnp.float32) + own.astype(jnp.float32) + edges.astype(jnp.float32) + spread

time: 128 us -> 91 us (0.71)
  Pallas kernels: 31.9 us -> 75.9 us
  waiting for transfers between devices: 31 us -> 0 us
  starting transfers between devices: 24 us -> 0 us
  blocking collectives: 20.7 us -> 0 us
  other arithmetic: 7.94 us -> 1.91 us
  local copies, waits for them, and re-layouts: 6.46 us -> 8.4 us
    pallas_call x0 -> x2, Pallas kernels: none -> 44 us  [the longest x1 24.9 us: local(): pl.pallas_call(functools.partial(exchange_in, groups, head_count, share,...]
    all_to_all x3 -> x0, waiting for transfers between devices: 27.6 us -> none  [the longest x1 21.3 us: local(): lax.all_to_all(sends, 'head', split_axis=0, concat_axis=0, tiled=True)]
    all_to_all x1 -> x0, blocking collectives: 20.7 us -> none  [local(): lax.all_to_all(result.reshape(head_count, share, width), 'head', split_ax...]
    all_to_all x3 -> x0, starting transfers between devices: 12.1 us -> none  [the longest x1 5.1 us: local(): lax.all_to_all(jnp.broadcast_to(piece[None, :], pieces.shape), 'tile', sp...]
    ppermute x6 -> x0, starting transfers between devices: 12 us -> none  [passed_along(): return lax.ppermute(value, axis, pairs)]
    ppermute x6 -> x0, waiting for transfers between devices: 3.34 us -> none  [passed_along(): return lax.ppermute(value, axis, pairs)]
    slice x2, local copies, waits for them, and re-layouts: 0.02 us -> 2.33 us  [the longest x1 1.19 us: local(): grad_in[:, h * rows:(h + 1) * rows]]
    broadcast_in_dim x1 -> x0, other arithmetic: 1.41 us -> none  [local(): jnp.broadcast_to(piece[None, :], pieces.shape)]
  transfers between devices with their start and end apart: 9 -> 0, of which waited for: 5 -> 0; matrix products, arithmetic and copies ran while one was open for 6% -> 0% of each run, Pallas kernels for 0% -> 0%
where the time goes in v2:
time: 91 us; the launch traced here: 90.7 us
  Pallas kernels  75.9 us (83%)
  local copies, waits for them, and re-layouts  8.4 us (9%)
  matrix products  3.7 us (4%)
  other arithmetic  1.91 us (2%)
    pallas_call x1, Pallas kernels, local(): pl.pallas_call(functools.partial(attention_body, rows, near, keys, grad_s...  31.9 us
    pallas_call x1, Pallas kernels, local(): pl.pallas_call(functools.partial(exchange_in, groups, head_count, share,...  24.9 us
    pallas_call x1, Pallas kernels, local(): pl.pallas_call(functools.partial(exchange_out, groups, head_count, share,...  19.1 us
    unnamed x16, local copies, waits for them, and re-layouts  4.76 us
    dot_general x1, matrix products, local(): lax.dot_general(answers.transpose(1, 0, 2).reshape(share, 3 * border), ch...  2.43 us

profile of v2, /device:TPU:0, one launch (start us, length us, event | category | flops | bytes accessed | tf_op | source)
XLA Modules:
  0.0 90.7 jit_solution(11108388486924191309)
XLA Ops:
  0.6 0.0 copy-start.2
  0.6 1.2 %fusion.22 = (bf16[64,1024]{1,0:T(8,128)(2,1)S(1)}, bf16[64,1024]{1,0:T(8,128)(2,1)S(1)}, bf16[64,1024]{1,0:T(8,128)(2,1)S(1)}, bf16[64,1024]{1,0:T(8,128)(2,1)S(1)}) fusion(bf16[64,4096]{1,0:T(8,128)(2,1)} %param.7), kind=kLoop, calls=%fused_computation.55 | loop fusion | bytes 1048576 | tf_op jit(solution)/shard_map/slice | solution.py:301
  1.8 1.1 %fusion.24 = (bf16[64,1152]{1,0:T(8,128)(2,1)S(1)}, bf16[64,1152]{1,0:T(8,128)(2,1)S(1)}) fusion(bf16[64,4096]{1,0:T(8,128)(2,1)} %param.6), kind=kLoop, calls=%fused_computation.57 | loop fusion | bytes 589824 | tf_op jit(solution)/shard_map/slice | solution.py:301
  3.0 0.0 copy-done.2
  3.0 0.1 fusion.23
  3.1 0.2 fusion.12
  3.2 0.0 copy-start.4
  3.2 0.0 copy-start.5
  3.3 0.0 copy-start.6
  3.3 0.2 pad_maximum_fusion.pieces
  3.5 0.7 copy-done.4
  4.1 0.0 copy-done.5
  4.2 0.0 copy-done.6
  4.2 1.3 %fusion.6 = bf16[8,3,8,128]{3,2,1,0:T(8,128)(2,1)S(1)} fusion(bf16[64,4096]{1,0:T(8,128)(2,1)S(1)} %copy-done.2, s32[384]{0:T(512)S(1)} %bitcast.71), kind=kOutput, calls=%fused_computation.7 | convolution fusion | flops 202924032 | bytes 574976 | tf_op jit(solution)/shard_map/dot_general | solution.py:294
  5.5 24.9 %exchange_in.1.recv = bf16[256,3584]{1,0:T(8,128)(2,1)S(1)} custom-call(bf16[4,64,2176]{2,1,0:T(8,128)(2,1)S(1)} %pad_maximum_fusion.pieces, bf16[3,64,128]{2,1,0:T(8,128)(2,1)S(1)} %bitcast.69, bf16[64,1024]{1,0:T(8,128)(2,1)S(1)} %pad_maximum_fusion.2.w), custom_call_target="tpu_custom_call" | custom-call | tf_op jit(solution)/shard_map/exchange_in/pallas_call | solution.py:309
  30.4 0.0 copy-start
  30.4 1.2 %copy-done = bf16[256,3584]{1,0:T(8,128)(2,1)} copy-done((bf16[256,3584]{1,0:T(8,128)(2,1)}, bf16[256,3584]{1,0:T(8,128)(2,1)S(1)}, u32[]{:S(2)}) %copy-start) | copy-done | bytes 1835032
  31.7 1.5 %fusion.15.picks = s32[9,1024]{1,0:T(8,128)} fusion(s32[9,4096]{1,0:T(8,128)} %param.10, s32[]{:T(128)S(6)} %select_n.23, s32[1024]{0:T(1024)S(1)} %fusion.18, s32[]{:T(128)S(6)} %mul.11), kind=kLoop, calls=%fused_computation.31 | loop fusion | flops 156672 | bytes 77832 | tf_op jit(solution)/shard_map/jit(_where)/select_n | solution.py:330
  33.2 31.9 %attend.1.result = bf16[256,2560]{1,0:T(8,128)(2,1)} custom-call(bf16[256,3584]{1,0:T(8,128)(2,1)} %copy-done, s32[9,1024]{1,0:T(8,128)} %fusion.15.picks), custom_call_target="tpu_custom_call" | custom-call | tf_op jit(solution)/shard_map/attend/pallas_call | solution.py:337
  65.1 0.0 copy-start.1
  65.1 1.3 %copy-done.1 = bf16[256,2560]{1,0:T(8,128)(2,1)S(1)} copy-done((bf16[256,2560]{1,0:T(8,128)(2,1)S(1)}, bf16[256,2560]{1,0:T(8,128)(2,1)}, u32[]{:S(2)}) %copy-start.1) | copy-done | bytes 1310744
  66.4 19.1 %exchange_out.1 = (bf16[4,64,1152]{2,1,0:T(8,128)(2,1)S(1)}, bf16[3,64,128]{2,1,0:T(8,128)(2,1)S(1)}, bf16[8,64,128]{2,1,0:T(8,128)(2,1)S(1)}) custom-call(bf16[256,2560]{1,0:T(8,128)(2,1)S(1)} %copy-done.1), custom_call_target="tpu_custom_call" | custom-call | tf_op jit(solution)/shard_map/exchange_out/pallas_call | solution.py:368
  85.5 0.0 copy-start.3
  85.5 0.1 slice_bitcast_fusion.8
  85.6 0.5 concatenate.36
  86.1 0.2 slice_bitcast_fusion.4
  86.3 0.2 copy-done.3
  86.5 2.4 %fusion.2 = f32[64,4096]{1,0:T(8,128)} fusion(s32[384]{0:T(512)S(1)} %bitcast.72, bf16[64,4096]{1,0:T(8,128)(2,1)S(1)} %concatenate.36, bf16[64,4096]{1,0:T(8,128)(2,1)S(1)} %copy-done.3, bf16[64,1024]{1,0:T(8,128)(2,1)S(1)} %get-tuple-element.13, bf16[64,1024]{1,0:T(8,128)(2,1)S(1)} %get-tuple-element.14, bf16[64,1024]{1,0:T(8,128)(2,1)S(1)} %get-tuple-element.15, ...), kind=kOutput, calls=%fused_computation.3 | convolution fusion | flops 206307328 | bytes 2672128 | tf_op jit(solution)/shard_map/dot_general | solution.py:412
  89.0 0.2 copy.11
  89.1 0.1 reshape.35
  89.3 0.7 copy.12
  90.0 0.1 slice.111
  90.1 0.6 copy.22
  (9 shorter events, 0.1 us)
Async XLA Ops:
  0.6 2.4 %copy-start.2 = (bf16[64,4096]{1,0:T(8,128)(2,1)S(1)}, bf16[64,4096]{1,0:T(8,128)(2,1)}, u32[]{:S(2)}) copy-start(bf16[64,4096]{1,0:T(8,128)(2,1)} %param.6) | copy-start | bytes 1572868
  3.2 0.9 copy-start.4
  3.2 0.9 copy-start.5
  3.3 0.9 copy-start.6
  30.4 1.3 %copy-start = (bf16[256,3584]{1,0:T(8,128)(2,1)}, bf16[256,3584]{1,0:T(8,128)(2,1)S(1)}, u32[]{:S(2)}) copy-start(bf16[256,3584]{1,0:T(8,128)(2,1)S(1)} %exchange_in.1.recv) | copy-start | bytes 5505028
  65.1 1.3 %copy-start.1 = (bf16[256,2560]{1,0:T(8,128)(2,1)S(1)}, bf16[256,2560]{1,0:T(8,128)(2,1)}, u32[]{:S(2)}) copy-start(bf16[256,2560]{1,0:T(8,128)(2,1)} %attend.1.result) | copy-start | bytes 3932164
  85.5 1.0 %copy-start.3 = (bf16[64,4096]{1,0:T(8,128)(2,1)S(1)}, bf16[64,4096]{1,0:T(8,128)(2,1)}, u32[]{:S(2)}) copy-start(bf16[64,4096]{1,0:T(8,128)(2,1)} %param.7) | copy-start | bytes 1572868
